TPU v7x, 512 devices: a whole 4x8x8 slice. The times are simulated.
512 devices in a mesh: row: 16 (over z, core), col: 32 (over x, y).
Axes of the slice: x: 4, y: 8, z: 8, core: 2. Of those that a mesh axis runs over, the one named last changes fastest.
Arguments:
- source_embed: float32 [64, 16384], P('col', 'row'), may hold values from -40 to 40
- target_embed: float32 [64, 32768], P('row', 'col'), may hold values from -40 to 40
- source_mass: float32 [16384], P('row'), may hold values from -2 to 2
- target_mass: float32 [32768], P('col'), may hold values from -2 to 2
- tile_list: int32 [16, 32, 2, 12], P('row', 'col'), may hold values from -1 to 127, as said below
- tile_counts: int32 [16, 32], P('row', 'col'), may hold values from 4 to 12, as said below
Outputs:
- source_potential: float32 [16384], P('row')
- target_potential: float32 [32768], P('col')
Inputs may be any that keep to these rules, and one draw needn't show every extreme that they name: `tile_list`: for the device at row index r and col index c, the slots below tile_counts[r, c] name distinct tiles whose row block lies in r * 4 to (r + 1) * 4 - 1 and whose column block lies in c * 4 to (c + 1) * 4 - 1; every row block and every column block of those ranges appears among them; the later slots hold -1 in both entries. `tile_counts`: some device has all 12 slots live.
All inputs are finite; a program needn't handle non-finite values.
Results may differ from a plain program's by a relative error of at most 0.0003.
Values sent between devices are 32-bit elements; how exact they have to be, the bound alone decides.
A program may use at most 64 MiB of HBM per device.

v0:
```python
import jax
import jax.numpy as jnp
from jax import lax
from jax.sharding import PartitionSpec as P

TILE = 256
ITERS = 3


entropic = 0.1
lowest = -1e30


def pair_combine(earlier, later):
    highest = jnp.maximum(earlier[0], later[0])
    return (
        highest,
        earlier[1] * jnp.exp(earlier[0] - highest) + later[1] * jnp.exp(later[0] - highest),
    )


def take_block(source_data, block):
    return lax.dynamic_slice_in_dim(source_data, block * TILE, TILE, source_data.ndim - 1)


def fold_block(running, offset, block_max, block_total, usable):
    previous = (
        lax.dynamic_slice_in_dim(running[0], offset, TILE),
        lax.dynamic_slice_in_dim(running[1], offset, TILE),
    )
    merged = pair_combine(previous, (block_max, block_total))
    new_max = jnp.where(usable, merged[0], previous[0])
    new_total = jnp.where(usable, merged[1], previous[1])
    return (
        lax.dynamic_update_slice_in_dim(running[0], new_max, offset, 0),
        lax.dynamic_update_slice_in_dim(running[1], new_total, offset, 0),
    )


def accumulate(
    running,
    sources,
    source_norms,
    targets,
    target_norms,
    potential,
    block_rows,
    block_cols,
    stop_slot,
    to_rows,
):
    per_turn = 4
    slot_total = block_rows.shape[0]
    features = sources.shape[0]
    turn_count = (stop_slot + per_turn - 1) // per_turn
    take_many = jax.vmap(take_block, in_axes=(None, 0))

    def one_turn(turn, running):
        slot_ids = turn * per_turn + jnp.arange(per_turn, dtype=jnp.int32)
        live_slots = slot_ids < stop_slot
        slot_ids = jnp.minimum(slot_ids, slot_total - 1)
        row_ids = block_rows[slot_ids]
        col_ids = block_cols[slot_ids]
        left_blocks = take_many(sources, row_ids)
        right_blocks = take_many(targets, col_ids)
        left_norms = take_many(source_norms, row_ids)
        right_norms = take_many(target_norms, col_ids)
        inner_products = lax.dot_general(
            left_blocks,
            right_blocks,
            (((1,), (1,)), ((0,), (0,))),
            precision=lax.Precision.HIGHEST,
            preferred_element_type=jnp.float32,
        )
        cost_tile = (left_norms[:, :, None] + right_norms[:, None, :] - 2.0 * inner_products) / (
            2.0 * features
        )
        if to_rows:
            values = take_many(potential, col_ids)
            scores = (values[:, None, :] - cost_tile) / entropic
            block_max = jnp.max(scores, axis=2)
            block_total = jnp.sum(jnp.exp(scores - block_max[:, :, None]), axis=2)
            offsets = row_ids * TILE
        else:
            values = take_many(potential, row_ids)
            scores = (values[:, :, None] - cost_tile) / entropic
            block_max = jnp.max(scores, axis=1)
            block_total = jnp.sum(jnp.exp(scores - block_max[:, None, :]), axis=1)
            offsets = col_ids * TILE
        for member in range(per_turn):
            running = fold_block(
                running, offsets[member], block_max[member], block_total[member], live_slots[member]
            )
        return running

    return lax.fori_loop(0, turn_count, one_turn, running)


def fresh_carry(length):
    return (jnp.full((length,), lowest, jnp.float32), jnp.zeros((length,), jnp.float32))


def reduce_rows(running):
    maxima = lax.pmax(running[0], "col")
    totals = lax.psum(running[1] * jnp.exp(running[0] - maxima), "col")
    return maxima + jnp.log(totals)


def reduce_cols(running):
    maxima = lax.pmax(running[0], "row")
    totals = lax.psum(running[1] * jnp.exp(running[0] - maxima), "row")
    return maxima + jnp.log(totals)


def shards(source_embed, target_embed, source_mass, target_mass, tile_list, tile_counts):
    sources = lax.all_gather(source_embed, "col", axis=0, tiled=True)
    targets = lax.all_gather(target_embed, "row", axis=0, tiled=True)
    source_norms = jnp.sum(sources * sources, axis=0)
    target_norms = jnp.sum(targets * targets, axis=0)
    row_blocks = sources.shape[1] // TILE
    col_blocks = targets.shape[1] // TILE
    row_first = lax.axis_index("row") * row_blocks
    col_first = lax.axis_index("col") * col_blocks
    own_count = tile_counts[0, 0]
    own_rows = jnp.maximum(tile_list[0, 0, 0] - row_first, 0)
    own_cols = jnp.maximum(tile_list[0, 0, 1] - col_first, 0)
    source_side = jnp.zeros((sources.shape[1],), jnp.float32)
    target_side = jnp.zeros((targets.shape[1],), jnp.float32)
    for iteration in range(ITERS):
        row_carry = accumulate(
            fresh_carry(sources.shape[1]),
            sources,
            source_norms,
            targets,
            target_norms,
            target_side,
            own_rows,
            own_cols,
            own_count,
            True,
        )
        source_side = entropic * (source_mass - reduce_rows(row_carry))
        column_carry = accumulate(
            fresh_carry(targets.shape[1]),
            sources,
            source_norms,
            targets,
            target_norms,
            source_side,
            own_rows,
            own_cols,
            own_count,
            False,
        )
        target_side = entropic * (target_mass - reduce_cols(column_carry))
    return (source_side, target_side)


def solution(mesh):
    in_specs = (
        P("col", "row"),
        P("row", "col"),
        P("row"),
        P("col"),
        P("row", "col", None, None),
        P("row", "col"),
    )
    out_specs = (P("row"), P("col"))
    return jax.shard_map(shards, mesh=mesh, in_specs=in_specs, out_specs=out_specs, check_vma=False)
```

profile of v0, /device:TPU:1, one launch (start us, length us, event | category | flops | bytes accessed | tf_op | source)
XLA Modules:
  0.0 1441.1 jit_solution(15978563129742898334)
XLA Ops:
  2.0 25.2 %all-gather.1 = f32[16,4,1024]{2,1,0:T(4,128)S(1)} all-gather(f32[1,4,1024]{2,1,0:T(4,128)S(1)} %bitcast.655), channel_id=1, replica_groups=mesh['row'=16,'col'=32] {'row'}, dimensions={0}, use_global_device_ids=true | all-gather | bytes 278528 | tf_op jit(solution)/shard_map/all_gather | solution.py:117
  28.0 38.2 %all-gather = f32[32,2,1024]{2,1,0:T(2,128)S(1)} all-gather(f32[1,2,1024]{2,1,0:T(2,128)S(1)} %bitcast.656), channel_id=1, replica_groups=mesh['row'=16,'col'=32] {'col'}, dimensions={0}, use_global_device_ids=true | all-gather | bytes 270336 | tf_op jit(solution)/shard_map/all_gather | solution.py:116
  67.1 79.1 %while.139 = (s32[]{:T(128)}, f32[1024]{0:T(1024)S(1)}, f32[1024]{0:T(1024)S(1)}, s32[]{:T(128)}, s32[]{:T(128)}, /*index=5*/s32[12]{0:T(128)S(1)}, s32[12]{0:T(...) while((s32[]{:T(128)}, f32[1024]{0:T(1024)S(1)}, ...), condition=%wide.region_5.6_spmd, body=%wide.region_2.5_spmd.sunk | while | flops 203693120 | bytes 3502546 | solution.py:96
  73.7 5.9 while.173
  86.1 5.9 while.172
  113.3 5.9 while.173
  125.7 5.9 while.172
  146.3 98.1 %pmax.42 = f32[1024]{0:T(1024)S(1)} all-reduce(f32[1024]{0:T(1024)S(1)} %get-tuple-element.381), channel_id=1, replica_groups=mesh['row'=16,'col'=32] {'col'}, use_global_device_ids=true, to_apply=%region_6.7 | all-reduce | flops 1024 | bytes 8192 | tf_op jit(solution)/shard_map/pmax | solution.py:104
  244.4 55.9 %psum.42 = f32[1024]{0:T(1024)S(1)} all-reduce(f32[1024]{0:T(1024)S(1)} %exponential_multiply_fusion.5), channel_id=1, replica_groups=mesh['row'=16,'col'=32] {'col'}, use_global_device_ids=true, to_apply=%region_7.8 | all-reduce | flops 1024 | bytes 8192 | tf_op jit(solution)/shard_map/psum | solution.py:105
  300.4 90.3 %while.145 = (s32[]{:T(128)}, f32[1024]{0:T(1024)S(1)}, f32[1024]{0:T(1024)S(1)}, s32[]{:T(128)}, s32[]{:T(128)}, /*index=5*/s32[12]{0:T(128)S(1)}, s32[12]{0:T(...) while((s32[]{:T(128)}, f32[1024]{0:T(1024)S(1)}, ...), condition=%wide.region_11.12_spmd, body=%wide.region_8.11_spmd.sunk | while | flops 203693120 | bytes 3503598 | solution.py:96
  313.5 5.9 while.177
  319.4 5.9 while.178
  325.3 5.9 while.179
  358.7 5.9 while.177
  364.5 5.9 while.178
  370.4 5.9 while.179
  390.7 107.2 %pmax.43 = f32[1024]{0:T(1024)S(1)} all-reduce(f32[1024]{0:T(1024)S(1)} %get-tuple-element.383), channel_id=1, replica_groups=mesh['row'=16,'col'=32] {'row'}, use_global_device_ids=true, to_apply=%region_12.13 | all-reduce | flops 1024 | bytes 8192 | tf_op jit(solution)/shard_map/pmax | solution.py:110
  497.9 23.6 %psum.43 = f32[1024]{0:T(1024)S(1)} all-reduce(f32[1024]{0:T(1024)S(1)} %exponential_multiply_fusion.4), channel_id=1, replica_groups=mesh['row'=16,'col'=32] {'row'}, use_global_device_ids=true, to_apply=%region_13.14 | all-reduce | flops 1024 | bytes 8192 | tf_op jit(solution)/shard_map/psum | solution.py:111
  521.5 90.3 %while.151 = (s32[]{:T(128)}, f32[1024]{0:T(1024)S(1)}, f32[1024]{0:T(1024)S(1)}, s32[]{:T(128)}, s32[]{:T(128)}, /*index=5*/s32[12]{0:T(128)S(1)}, s32[12]{0:T(...) while((s32[]{:T(128)}, f32[1024]{0:T(1024)S(1)}, ...), condition=%wide.region_17.18_spmd, body=%wide.region_14.17_spmd.sunk | while | flops 203693120 | bytes 3503598 | solution.py:96
  534.6 5.9 while.182
  540.5 5.9 while.183
  546.4 5.9 while.184
  579.8 5.9 while.182
  585.7 5.9 while.183
  591.5 5.9 while.184
  611.8 64.3 %pmax.44 = f32[1024]{0:T(1024)S(1)} all-reduce(f32[1024]{0:T(1024)S(1)} %get-tuple-element.385), channel_id=1, replica_groups=mesh['row'=16,'col'=32] {'col'}, use_global_device_ids=true, to_apply=%region_18.19 | all-reduce | flops 1024 | bytes 8192 | tf_op jit(solution)/shard_map/pmax | solution.py:104
  676.1 56.1 %psum.44 = f32[1024]{0:T(1024)S(1)} all-reduce(f32[1024]{0:T(1024)S(1)} %exponential_multiply_fusion.3), channel_id=1, replica_groups=mesh['row'=16,'col'=32] {'col'}, use_global_device_ids=true, to_apply=%region_19.20 | all-reduce | flops 1024 | bytes 8192 | tf_op jit(solution)/shard_map/psum | solution.py:105
  732.3 90.3 %while.157 = (s32[]{:T(128)}, f32[1024]{0:T(1024)S(1)}, f32[1024]{0:T(1024)S(1)}, s32[]{:T(128)}, s32[]{:T(128)}, /*index=5*/s32[12]{0:T(128)S(1)}, s32[12]{0:T(...) while((s32[]{:T(128)}, f32[1024]{0:T(1024)S(1)}, ...), condition=%wide.region_23.24_spmd, body=%wide.region_20.23_spmd.sunk | while | flops 203693120 | bytes 3503598 | solution.py:96
  745.4 5.9 while.187
  751.3 5.9 while.188
  757.1 5.9 while.189
  790.5 5.9 while.187
  796.4 5.9 while.188
  802.3 5.9 while.189
  822.6 134.9 %pmax.45 = f32[1024]{0:T(1024)S(1)} all-reduce(f32[1024]{0:T(1024)S(1)} %get-tuple-element.387), channel_id=1, replica_groups=mesh['row'=16,'col'=32] {'row'}, use_global_device_ids=true, to_apply=%region_24.25 | all-reduce | flops 1024 | bytes 8192 | tf_op jit(solution)/shard_map/pmax | solution.py:110
  957.5 23.5 %psum.45 = f32[1024]{0:T(1024)S(1)} all-reduce(f32[1024]{0:T(1024)S(1)} %exponential_multiply_fusion.2), channel_id=1, replica_groups=mesh['row'=16,'col'=32] {'row'}, use_global_device_ids=true, to_apply=%region_25.26 | all-reduce | flops 1024 | bytes 8192 | tf_op jit(solution)/shard_map/psum | solution.py:111
  981.1 90.3 %while.163 = (s32[]{:T(128)}, f32[1024]{0:T(1024)S(1)}, f32[1024]{0:T(1024)S(1)}, s32[]{:T(128)}, s32[]{:T(128)}, /*index=5*/s32[12]{0:T(128)S(1)}, s32[12]{0:T(...) while((s32[]{:T(128)}, f32[1024]{0:T(1024)S(1)}, ...), condition=%wide.region_29.30_spmd, body=%wide.region_26.29_spmd.sunk | while | flops 203693120 | bytes 3503598 | solution.py:96
  994.2 5.9 while.192
  1000.1 5.9 while.193
  1006.0 5.9 while.194
  1039.4 5.9 while.192
  1045.3 5.9 while.193
  1051.1 5.9 while.194
  1071.4 56.1 %pmax.46 = f32[1024]{0:T(1024)S(1)} all-reduce(f32[1024]{0:T(1024)S(1)} %get-tuple-element.389), channel_id=1, replica_groups=mesh['row'=16,'col'=32] {'col'}, use_global_device_ids=true, to_apply=%region_30.31 | all-reduce | flops 1024 | bytes 8192 | tf_op jit(solution)/shard_map/pmax | solution.py:104
  1127.5 56.9 %psum.46 = f32[1024]{0:T(1024)S(1)} all-reduce(f32[1024]{0:T(1024)S(1)} %exponential_multiply_fusion.1), channel_id=1, replica_groups=mesh['row'=16,'col'=32] {'col'}, use_global_device_ids=true, to_apply=%region_31.32 | all-reduce | flops 1024 | bytes 8192 | tf_op jit(solution)/shard_map/psum | solution.py:105
  1184.5 90.3 %while.169 = (s32[]{:T(128)}, f32[1024]{0:T(1024)S(1)}, f32[1024]{0:T(1024)S(1)}, s32[]{:T(128)}, s32[]{:T(128)}, /*index=5*/s32[12]{0:T(128)S(1)}, s32[12]{0:T(...) while((s32[]{:T(128)}, f32[1024]{0:T(1024)S(1)}, ...), condition=%wide.region_35.36_spmd, body=%wide.region_32.35_spmd.sunk | while | flops 203693120 | bytes 3503598 | solution.py:96
  1274.8 142.1 %pmax.47 = f32[1024]{0:T(1024)S(1)} all-reduce(f32[1024]{0:T(1024)S(1)} %get-tuple-element.391), channel_id=1, replica_groups=mesh['row'=16,'col'=32] {'row'}, use_global_device_ids=true, to_apply=%region_36.37 | all-reduce | flops 1024 | bytes 8192 | tf_op jit(solution)/shard_map/pmax | solution.py:110
  1416.9 23.6 %psum.47 = f32[1024]{0:T(1024)S(1)} all-reduce(f32[1024]{0:T(1024)S(1)} %exponential_multiply_fusion), channel_id=1, replica_groups=mesh['row'=16,'col'=32] {'row'}, use_global_device_ids=true, to_apply=%region_37.38 | all-reduce | flops 1024 | bytes 8192 | tf_op jit(solution)/shard_map/psum | solution.py:111
  (1085 shorter events, 614.7 us)
Async XLA Ops:
  1.3 0.7 copy-start.3
  27.3 0.7 copy-start.4
  66.4 0.7 copy-start.5
  244.4 55.9 %copy-start.1 = (f32[1024]{0:T(1024)S(1)}, f32[1024]{0:T(1024)}, u32[]{:S(2)}) copy-start(f32[1024]{0:T(1024)} %param.20) | copy-start | bytes 12292
  497.9 23.6 %copy-start.2 = (f32[1024]{0:T(1024)S(1)}, f32[1024]{0:T(1024)}, u32[]{:S(2)}) copy-start(f32[1024]{0:T(1024)} %param.21) | copy-start | bytes 12292
  1274.8 142.1 %copy-start = (f32[1024]{0:T(1024)}, f32[1024]{0:T(1024)S(1)}, u32[]{:S(2)}) copy-start(f32[1024]{0:T(1024)S(1)} %get-tuple-element.3983) | copy-start | bytes 12292
where the time goes:
time: 1450 us; the launch traced here: 1440 us
  blocking collectives  906 us (62%)
  local copies, waits for them, and re-layouts  372 us (26%)
  loops' own time  95.3 us (7%)
  other arithmetic  51.9 us (4%)
  matrix products  14.9 us (1%)
    pmax x3, blocking collectives, reduce_cols(): maxima = lax.pmax(running[0], 'row')  384 us
    gather x712, local copies, waits for them, and re-layouts  337 us
    pmax x3, blocking collectives, reduce_rows(): maxima = lax.pmax(running[0], 'col')  219 us
    psum x3, blocking collectives, reduce_rows(): totals = lax.psum(running[1] * jnp.exp(running[0] - maxima), 'col')  169 us
    another operation x6, loops' own time, accumulate(): return lax.fori_loop(0, turn_count, one_turn, running)  92.1 us
    psum x3, blocking collectives, reduce_cols(): totals = lax.psum(running[1] * jnp.exp(running[0] - maxima), 'row')  70.6 us
    dynamic_update_slice x48, other arithmetic, fold_block(): lax.dynamic_update_slice_in_dim(running[1], new_total, offset, 0)  41 us
    all_gather x1, blocking collectives, shards(): sources = lax.all_gather(source_embed, 'col', axis=0, tiled=True)  38.2 us

commit v1 on v0

v1 whole, which is shorter than its diff:
```python
import functools
import math

import jax
import jax.numpy as jnp
from jax import lax
from jax.experimental import pallas as pl
from jax.experimental.pallas import tpu as pltpu
from jax.sharding import PartitionSpec as P

TILE = 256
ITERS = 3
RING_Y = 8
CORES = 2
SPAN = 32

entropic = 0.1
dead_cost = 1e30
log2e = math.log2(math.e)
MESH = pl.DeviceIdType.MESH
LANES = 128


def ring_offsets(size):
    return sorted(range(1, size), key=lambda k: -min(k, size - k))


def wait_bytes(ref, sem):
    pltpu.make_async_copy(ref, ref, sem).wait()


def split_three(x):
    high = x.astype(jnp.bfloat16)
    rest = x - high.astype(jnp.float32)
    middle = rest.astype(jnp.bfloat16)
    low = (rest - middle.astype(jnp.float32)).astype(jnp.bfloat16)
    return high, middle, low


def combine(parts):
    highest = functools.reduce(jnp.maximum, parts)
    total = functools.reduce(jnp.add, [jnp.exp2(part - highest) for part in parts])
    return highest + jnp.log2(total)


def make_kernel(n_row, n_col, ring_y, cells, dim):
    ring_x = n_col // ring_y
    ring_z = n_row // CORES
    blocks = cells // LANES
    src_rows = dim // n_col
    tgt_rows = dim // n_row
    per = max(src_rows, tgt_rows)
    steps = dim // per
    tiles = cells // TILE
    x_offsets = ring_offsets(ring_x)
    y_offsets = ring_offsets(ring_y)
    z_offsets = [(0, 1)] + [(dz, dc) for dz in range(1, ring_z) for dc in range(CORES)]
    z_offsets.sort(key=lambda o: -min(o[0], ring_z - o[0]))

    def kernel(
        src_ref,
        tgt_ref,
        smass_ref,
        tmass_ref,
        list_ref,
        count_ref,
        out_ref,
        gsrc,
        gtgt,
        left,
        right,
        cost,
        cost_t,
        penalty,
        spread,
        part_x,
        part_y,
        part_z,
        got_x,
        got_y,
        got_z,
        gather_send,
        gather_recv,
        send_x,
        send_y,
        send_z,
        recv_x,
        recv_y,
        recv_z,
    ):
        row = lax.axis_index("row")
        col = lax.axis_index("col")
        x, y = col // ring_y, col % ring_y
        z, core = row // CORES, row % CORES
        x_peers = [(row, (x + dx) % ring_x * ring_y + y) for dx in x_offsets]
        y_peers = [(row, x * ring_y + (y + dy) % ring_y) for dy in y_offsets]
        z_peers = [((z + dz) % ring_z * CORES + (core + dc) % CORES, col) for dz, dc in z_offsets]

        barrier = pltpu.get_barrier_semaphore()
        for peer in y_peers + z_peers + x_peers:
            pl.semaphore_signal(barrier, inc=1, device_id=peer, device_id_type=MESH)

        own_src = gsrc.at[pl.ds(col * (blocks * src_rows), blocks * src_rows)]
        own_tgt = gtgt.at[pl.ds(row * (blocks * tgt_rows), blocks * tgt_rows)]
        for b in range(blocks):
            own_src[b * src_rows : (b + 1) * src_rows, :] = src_ref[:, b * LANES : (b + 1) * LANES]
            own_tgt[b * tgt_rows : (b + 1) * tgt_rows, :] = tgt_ref[:, b * LANES : (b + 1) * LANES]

        pl.semaphore_wait(barrier, len(x_peers) + len(y_peers) + len(z_peers))

        def send(src, dst, send_sem, recv_sem, peer):
            pltpu.make_async_remote_copy(
                src_ref=src,
                dst_ref=dst,
                send_sem=send_sem,
                recv_sem=recv_sem,
                device_id=peer,
                device_id_type=MESH,
            ).start()

        for peer in y_peers:
            send(own_src, own_src, gather_send.at[0], gather_recv.at[0], peer)
        for peer in z_peers:
            send(own_tgt, own_tgt, gather_send.at[1], gather_recv.at[1], peer)

        slots = list_ref[0, 0]
        slot_count = slots.shape[1]
        tile_ids = (slots[0:1, :] - row * tiles) * tiles + (slots[1:2, :] - col * tiles)
        live = lax.broadcasted_iota(jnp.int32, (1, slot_count), 1) < count_ref[...]
        tile_ids = jnp.where(live, tile_ids, -1)
        wanted = lax.broadcasted_iota(jnp.int32, (tiles * tiles * 8, slot_count), 0) // 8
        hits = jnp.where(wanted == tile_ids, 1.0, 0.0)
        found = jnp.max(hits, axis=1, keepdims=True)
        penalty[...] = jnp.broadcast_to(jnp.where(found > 0.5, 0.0, dead_cost), penalty.shape)

        unit = log2e / (entropic * 2.0 * dim)

        def load_features(ref, b, rows):
            found = []
            for q in range(per):
                start = q // rows * (blocks * rows) + b * rows + q % rows
                found.append(ref[pl.Slice(start, steps, per * blocks), :])
            return jnp.concatenate(found, axis=0)

        depth = left.shape[0]
        extra_rows = depth - 6 * dim

        def operands(gathered, out, rows, scale, is_left):
            for b in range(blocks):
                lanes = slice(b * LANES, (b + 1) * LANES)
                values = load_features(gathered, b, rows)
                norms = jnp.sum(values * values, axis=0, keepdims=True) * unit
                high, middle, low = split_three(values * scale if scale != 1.0 else values)
                order = (high, high, middle, middle, high, low)
                if not is_left:
                    order = (high, middle, high, middle, low, high)
                for k, term in enumerate(order):
                    out[k * dim : (k + 1) * dim, lanes] = term
                parts = [p.astype(jnp.float32) for p in split_three(norms)]
                one = jnp.ones((1, LANES), jnp.float32)
                pieces = parts + [one] * 3 if is_left else [one] * 3 + parts
                index = lax.broadcasted_iota(jnp.int32, (extra_rows, LANES), 0)
                extra = jnp.zeros((extra_rows, LANES), jnp.float32)
                for k, piece in enumerate(pieces):
                    extra = jnp.where(index == k, piece, extra)
                out[6 * dim :, lanes] = extra.astype(jnp.bfloat16)

        def fill(dst, lhs, rhs, major, minor):
            def one_row(rb, carry):
                rows = pl.ds(pl.multiple_of(rb * TILE, TILE), TILE)
                block = lhs[:, rows]
                for cb in range(tiles):
                    product = lax.dot_general(
                        block,
                        rhs[:, cb * TILE : (cb + 1) * TILE],
                        (((0,), (0,)), ((), ())),
                        preferred_element_type=jnp.float32,
                    )
                    tile = rb * major + cb * minor
                    extra = penalty[pl.ds(pl.multiple_of(tile * 8, 8), 8), :]
                    dst[rows, cb * TILE : (cb + 1) * TILE] = product + jnp.broadcast_to(
                        extra[0:1, 0:1], product.shape
                    )
                return carry

            lax.fori_loop(0, tiles, one_row, 0)

        def local_lse(costs, potential):
            turned = potential.T
            for b in range(blocks):
                spread[b * LANES : (b + 1) * LANES, :] = jnp.broadcast_to(
                    turned[:, b : b + 1], (LANES, LANES)
                )

            def fold(values, op):
                return op(values.reshape(SPAN // 8, 8, LANES), axis=0)

            def max_step(g, carry):
                rows = pl.ds(pl.multiple_of(g * SPAN, SPAN), SPAN)
                shift = spread[rows, :]
                return tuple(
                    jnp.maximum(
                        carry[b],
                        fold(shift - costs[rows, b * LANES : (b + 1) * LANES], jnp.max),
                    )
                    for b in range(blocks)
                )

            start = tuple(jnp.full((8, LANES), -3e38, jnp.float32) for b in range(blocks))
            maxima = lax.fori_loop(0, cells // SPAN, max_step, start)
            maxima = tuple(
                jnp.broadcast_to(jnp.max(m, axis=0, keepdims=True), (8, LANES)) for m in maxima
            )
            tall = tuple(jnp.broadcast_to(m[0:1], (SPAN, LANES)) for m in maxima)

            def sum_step(g, carry):
                rows = pl.ds(pl.multiple_of(g * SPAN, SPAN), SPAN)
                shift = spread[rows, :]
                return tuple(
                    carry[b]
                    + fold(
                        jnp.exp2((shift - costs[rows, b * LANES : (b + 1) * LANES]) - tall[b]),
                        jnp.sum,
                    )
                    for b in range(blocks)
                )

            start = tuple(jnp.zeros((8, LANES), jnp.float32) for b in range(blocks))
            totals = lax.fori_loop(0, cells // SPAN, sum_step, start)
            index = lax.broadcasted_iota(jnp.int32, (blocks, LANES), 0)
            highest = jnp.zeros((blocks, LANES), jnp.float32)
            total = jnp.ones((blocks, LANES), jnp.float32)
            for b in range(blocks):
                highest = jnp.where(index == b, maxima[b][0:1], highest)
                total = jnp.where(index == b, jnp.sum(totals[b], axis=0, keepdims=True), total)
            return highest + jnp.log2(total)

        wait_bytes(gsrc.at[pl.ds(0, len(y_peers) * blocks * src_rows)], gather_recv.at[0])
        group = ring_y * blocks * src_rows
        own_group = gsrc.at[pl.ds(x * group, group)]
        for peer in x_peers:
            send(own_group, own_group, gather_send.at[2], gather_recv.at[2], peer)
        wait_bytes(gtgt.at[pl.ds(0, len(z_peers) * blocks * tgt_rows)], gather_recv.at[1])
        operands(gtgt, right, tgt_rows, 1.0, False)
        wait_bytes(gsrc.at[pl.ds(0, len(x_peers) * group)], gather_recv.at[2])
        operands(gsrc, left, src_rows, -2.0 * unit, True)
        fill(cost_t, right, left, 1, tiles)

        source_mass = smass_ref[...] * log2e
        target_mass = tmass_ref[...] * log2e

        def iterate(turn, carry):
            target_side = carry[1]
            part_x[turn] = local_lse(cost_t, target_side)
            for k, peer in enumerate(x_peers):
                send(part_x.at[turn], got_x.at[turn, k], send_x, recv_x.at[turn], peer)

            @pl.when(turn == 0)
            def fill_cost():
                fill(cost, left, right, tiles, 1)

            wait_bytes(got_x.at[turn], recv_x.at[turn])
            part_y[turn] = combine([part_x[turn]] + [got_x[turn, k] for k in range(len(x_peers))])
            for k, peer in enumerate(y_peers):
                send(part_y.at[turn], got_y.at[turn, k], send_y, recv_y.at[turn], peer)
            wait_bytes(got_y.at[turn], recv_y.at[turn])
            lse = combine([part_y[turn]] + [got_y[turn, k] for k in range(len(y_peers))])
            source_side = source_mass - lse

            part_z[turn] = local_lse(cost, source_side)
            for k, peer in enumerate(z_peers):
                send(part_z.at[turn], got_z.at[turn, k], send_z, recv_z.at[turn], peer)
            wait_bytes(got_z.at[turn], recv_z.at[turn])
            lse = combine([part_z[turn]] + [got_z[turn, k] for k in range(len(z_peers))])
            return source_side, target_mass - lse

        zero = jnp.zeros((blocks, LANES), jnp.float32)
        source_side, target_side = lax.fori_loop(0, ITERS, iterate, (zero, zero))
        out_ref[0] = source_side
        out_ref[1] = target_side

        wait_bytes(gsrc.at[pl.ds(0, len(y_peers) * blocks * src_rows)], gather_send.at[0])
        wait_bytes(gtgt.at[pl.ds(0, len(z_peers) * blocks * tgt_rows)], gather_send.at[1])
        wait_bytes(gsrc.at[pl.ds(0, len(x_peers) * group)], gather_send.at[2])
        wait_bytes(got_x, send_x)
        wait_bytes(got_y, send_y)
        wait_bytes(got_z, send_z)

    def vector(count):
        return pltpu.VMEM((ITERS, count, blocks, LANES), jnp.float32)

    depth = 6 * dim + LANES
    scratch = [
        pltpu.VMEM((dim * blocks, LANES), jnp.float32),
        pltpu.VMEM((dim * blocks, LANES), jnp.float32),
        pltpu.VMEM((depth, cells), jnp.bfloat16),
        pltpu.VMEM((depth, cells), jnp.bfloat16),
        pltpu.VMEM((cells, cells), jnp.float32),
        pltpu.VMEM((cells, cells), jnp.float32),
        pltpu.VMEM((tiles * tiles * 8, LANES), jnp.float32),
        pltpu.VMEM((cells, LANES), jnp.float32),
        pltpu.VMEM((ITERS, blocks, LANES), jnp.float32),
        pltpu.VMEM((ITERS, blocks, LANES), jnp.float32),
        pltpu.VMEM((ITERS, blocks, LANES), jnp.float32),
        vector(len(x_offsets)),
        vector(len(y_offsets)),
        vector(len(z_offsets)),
        pltpu.SemaphoreType.DMA((3,)),
        pltpu.SemaphoreType.DMA((3,)),
        pltpu.SemaphoreType.DMA,
        pltpu.SemaphoreType.DMA,
        pltpu.SemaphoreType.DMA,
        pltpu.SemaphoreType.DMA((ITERS,)),
        pltpu.SemaphoreType.DMA((ITERS,)),
        pltpu.SemaphoreType.DMA((ITERS,)),
    ]
    return kernel, scratch


def shards(n_row, n_col, source_embed, target_embed, source_mass, target_mass, tile_list, tile_counts):
    cells = source_embed.shape[1]
    dim = source_embed.shape[0] * n_col
    blocks = cells // LANES
    kernel, scratch = make_kernel(n_row, n_col, RING_Y, cells, dim)
    whole = pl.BlockSpec(memory_space=pltpu.VMEM)
    sides = pl.pallas_call(
        kernel,
        out_shape=jax.ShapeDtypeStruct((2, blocks, LANES), jnp.float32),
        in_specs=[whole] * 6,
        out_specs=whole,
        scratch_shapes=scratch,
        compiler_params=pltpu.CompilerParams(collective_id=0, has_side_effects=True),
        name="sinkhorn",
    )(
        source_embed,
        target_embed,
        source_mass.reshape(blocks, LANES),
        target_mass.reshape(blocks, LANES),
        tile_list,
        tile_counts,
    )
    sides = sides * (entropic / log2e)
    return sides[0].reshape(cells), sides[1].reshape(cells)


def solution(mesh):
    in_specs = (
        P("col", "row"),
        P("row", "col"),
        P("row"),
        P("col"),
        P("row", "col", None, None),
        P("row", "col"),
    )
    out_specs = (P("row"), P("col"))
    body = functools.partial(shards, mesh.shape["row"], mesh.shape["col"])
    return jax.shard_map(body, mesh=mesh, in_specs=in_specs, out_specs=out_specs, check_vma=False)
```

time: 1450 us -> 80.2 us (0.06)
  blocking collectives: 906 us -> 0 us
  local copies, waits for them, and re-layouts: 372 us -> 0.6 us
  loops' own time: 95.3 us -> 0 us
  Pallas kernels: 0 us -> 77.3 us
  other arithmetic: 51.9 us -> 0.7 us
  matrix products: 14.9 us -> 0 us
    pmax x6 -> x0, blocking collectives: 603 us -> none  [the longest x3 384 us: reduce_cols(): maxima = lax.pmax(running[0], 'row')]
    gather x736 -> x0, local copies, waits for them, and re-layouts: 353 us -> none
    psum x6 -> x0, blocking collectives: 240 us -> none  [the longest x3 169 us: reduce_rows(): totals = lax.psum(running[1] * jnp.exp(running[0] - maxima), 'col')]
    another operation x66 -> x0, loops' own time: 95.3 us -> none  [the longest x6 92.1 us: accumulate(): return lax.fori_loop(0, turn_count, one_turn, running)]
    pallas_call x0 -> x1, Pallas kernels: none -> 77.3 us  [shards(): pl.pallas_call(kernel, out_shape=jax.ShapeDtypeStruct((2, blocks, LANES),...]
    all_gather x2 -> x0, blocking collectives: 63.4 us -> none  [the longest x1 38.2 us: shards(): sources = lax.all_gather(source_embed, 'col', axis=0, tiled=True)]
    dynamic_update_slice x48 -> x0, other arithmetic: 41 us -> none  [fold_block(): lax.dynamic_update_slice_in_dim(running[1], new_total, offset, 0)]
    slice x48 -> x0, local copies, waits for them, and re-layouts: 16 us -> none  [the longest x12 8.05 us: one_turn(): offsets[member]]
where the time goes in v1:
time: 80.2 us; the launch traced here: 79.9 us
  Pallas kernels  77.3 us (96%)
  between operations  1.29 us (2%)
    pallas_call x1, Pallas kernels, shards(): pl.pallas_call(kernel, out_shape=jax.ShapeDtypeStruct((2, blocks, LANES),...  77.3 us

profile of v1, /device:TPU:1, one launch (start us, length us, event | category | flops | bytes accessed | tf_op | source)
XLA Modules:
  0.0 79.9 jit_solution(9813206576847203336)
XLA Ops:
  1.3 77.3 %sinkhorn.1 = f32[2,8,128]{2,1,0:T(8,128)} custom-call(f32[2,1024]{1,0:T(2,128)} %src_ref.1, f32[4,1024]{1,0:T(4,128)} %tgt_ref.1, f32[8,128]{1,0:T(8,128)} %bitcast.6, f32[8,128]{1,0:T(8,128)} %bitcast.7, s32[1,1,2,12]{3,2,1,0:T(2,128)} %list_ref.1, s32[1,1]{1,0:T(1,128)S(6)} %copy.8.count_ref), custom_call_target="tpu_custom_call" | custom-call | tf_op jit(solution)/shard_map/sinkhorn/pallas_call | solution.py:326
  78.6 0.7 broadcast_multiply_fusion
  79.3 0.6 slice_bitcast_fusion

commit v2 on v1

v2 whole, which is shorter than its diff:
```python
import functools
import math

import jax
import jax.numpy as jnp
from jax import lax
from jax.experimental import pallas as pl
from jax.experimental.pallas import tpu as pltpu
from jax.sharding import PartitionSpec as P

TILE = 256
ITERS = 3
RING_Y = 8
CORES = 2
SPAN = 64
UNROLL = 4

entropic = 0.1
dead_cost = 1e30
log2e = math.log2(math.e)
MESH = pl.DeviceIdType.MESH
LANES = 128


def blocks_of(cells):
    return cells // LANES


def ring_offsets(size):
    return sorted(range(1, size), key=lambda k: -min(k, size - k))


def wait_bytes(ref, sem):
    pltpu.make_async_copy(ref, ref, sem).wait()


def split_three(x):
    high = x.astype(jnp.bfloat16)
    rest = x - high.astype(jnp.float32)
    middle = rest.astype(jnp.bfloat16)
    low = (rest - middle.astype(jnp.float32)).astype(jnp.bfloat16)
    return high, middle, low


def combine(parts):
    highest = functools.reduce(jnp.maximum, parts)
    total = functools.reduce(jnp.add, [jnp.exp2(part - highest) for part in parts])
    return highest + jnp.log2(total)


def make_kernel(n_row, n_col, ring_y, cells, dim, slot_count):
    ring_x = n_col // ring_y
    ring_z = n_row // CORES
    blocks = blocks_of(cells)
    src_rows = dim // n_col
    tgt_rows = dim // n_row
    per = max(src_rows, tgt_rows)
    steps = dim // per
    src_size = src_rows * blocks_of(cells)
    tgt_size = tgt_rows * blocks_of(cells)
    tiles = cells // TILE
    x_offsets = ring_offsets(ring_x)
    y_offsets = ring_offsets(ring_y)
    z_offsets = [(0, 1)] + [(dz, dc) for dz in range(1, ring_z) for dc in range(CORES)]
    z_offsets.sort(key=lambda o: -min(o[0], ring_z - o[0]))
    chain_offsets = ring_offsets(ring_z)
    plane_offsets = [(dx, dy) for dx in range(ring_x) for dy in range(ring_y) if dx or dy]
    plane_offsets.sort(key=lambda o: -min(o[0], ring_x - o[0]) - min(o[1], ring_y - o[1]))

    def kernel(
        src_hbm,
        tgt_hbm,
        smass_hbm,
        tmass_hbm,
        list_hbm,
        count_hbm,
        source_out,
        target_out,
        src_ref,
        tgt_ref,
        smass_ref,
        tmass_ref,
        list_ref,
        count_ref,
        gsrc,
        gtgt,
        left,
        right,
        cost,
        cost_t,
        penalty,
        spread,
        part_row,
        part_col,
        got_row,
        got_col,
        load_sem,
        gather_send,
        y_recv,
        z_recv,
        x_recv,
        pair_recv,
        row_send,
        col_send,
        row_recv,
        col_recv,
    ):
        row = lax.axis_index("row")
        col = lax.axis_index("col")
        x, y = col // ring_y, col % ring_y
        z, core = row // CORES, row % CORES
        x_peers = [(row, (x + dx) % ring_x * ring_y + y) for dx in x_offsets]
        y_peers = [(row, x * ring_y + (y + dy) % ring_y) for dy in y_offsets]
        chain_peers = [((z + dz) % ring_z * CORES + core, col) for dz in chain_offsets]
        partner = (z * CORES + (core + 1) % CORES, col)
        z_peers = [((z + dz) % ring_z * CORES + (core + dc) % CORES, col) for dz, dc in z_offsets]
        plane_peers = [
            (row, (x + dx) % ring_x * ring_y + (y + dy) % ring_y) for dx, dy in plane_offsets
        ]

        loads = [
            pltpu.make_async_copy(hbm, ref, load_sem.at[k])
            for k, (hbm, ref) in enumerate(
                [
                    (src_hbm, src_ref),
                    (tgt_hbm, tgt_ref),
                    (smass_hbm, smass_ref),
                    (tmass_hbm, tmass_ref),
                    (list_hbm, list_ref),
                    (count_hbm, count_ref),
                ]
            )
        ]
        for load in loads:
            load.start()
        barrier = pltpu.get_barrier_semaphore()
        greeted = y_peers + z_peers + x_peers
        for peer in greeted:
            pl.semaphore_signal(barrier, inc=1, device_id=peer, device_id_type=MESH)

        def src_chunk(owner):
            return gsrc.at[pl.ds(pl.multiple_of(owner * src_size, src_size), src_size)]

        def tgt_chunk(owner):
            return gtgt.at[pl.ds(pl.multiple_of(owner * tgt_size, tgt_size), tgt_size)]

        own_src = src_chunk(col)
        own_tgt = tgt_chunk(row)
        for load in loads:
            load.wait()
        for b in range(blocks):
            own_src[b * src_rows : (b + 1) * src_rows, :] = src_ref[:, b * LANES : (b + 1) * LANES]
            own_tgt[b * tgt_rows : (b + 1) * tgt_rows, :] = tgt_ref[:, b * LANES : (b + 1) * LANES]

        pl.semaphore_wait(barrier, len(greeted))

        def send(src, dst, send_sem, recv_sem, peer):
            pltpu.make_async_remote_copy(
                src_ref=src,
                dst_ref=dst,
                send_sem=send_sem,
                recv_sem=recv_sem,
                device_id=peer,
                device_id_type=MESH,
            ).start()

        for k, peer in enumerate(y_peers):
            send(own_src, own_src, gather_send.at[0], y_recv.at[k], peer)
        for k, peer in enumerate(chain_peers):
            send(own_tgt, own_tgt, gather_send.at[1], z_recv.at[k], peer)
        for peer in x_peers:
            send(own_src, own_src, gather_send.at[2], x_recv, peer)
        send(own_tgt, own_tgt, gather_send.at[3], pair_recv, partner)

        slots = list_ref[0, 0]
        tile_ids = (slots[0:1, :] - row * tiles) * tiles + (slots[1:2, :] - col * tiles)
        live = lax.broadcasted_iota(jnp.int32, (1, slot_count), 1) < count_ref[...]
        tile_ids = jnp.where(live, tile_ids, -1)
        wanted = lax.broadcasted_iota(jnp.int32, (tiles * tiles * 8, slot_count), 0) // 8
        hits = jnp.where(wanted == tile_ids, 1.0, 0.0)
        found = jnp.max(hits, axis=1, keepdims=True)
        penalty[...] = jnp.broadcast_to(jnp.where(found > 0.5, 0.0, dead_cost), penalty.shape)

        unit = log2e / (entropic * 2.0 * dim)

        def load_features(ref, b, rows):
            found = []
            for q in range(per):
                start = q // rows * (blocks * rows) + b * rows + q % rows
                found.append(ref[pl.Slice(start, steps, per * blocks), :])
            return jnp.concatenate(found, axis=0)

        depth = left.shape[0]
        extra_rows = depth - 6 * dim

        def operands(gathered, out, rows, scale, is_left):
            for b in range(blocks):
                lanes = slice(b * LANES, (b + 1) * LANES)
                values = load_features(gathered, b, rows)
                norms = jnp.sum(values * values, axis=0, keepdims=True) * unit
                high, middle, low = split_three(values * scale if scale != 1.0 else values)
                order = (high, high, middle, middle, high, low)
                if not is_left:
                    order = (high, middle, high, middle, low, high)
                for k, term in enumerate(order):
                    out[k * dim : (k + 1) * dim, lanes] = term
                parts = [p.astype(jnp.float32) for p in split_three(norms)]
                one = jnp.ones((1, LANES), jnp.float32)
                pieces = parts + [one] * 3 if is_left else [one] * 3 + parts
                index = lax.broadcasted_iota(jnp.int32, (extra_rows, LANES), 0)
                extra = jnp.zeros((extra_rows, LANES), jnp.float32)
                for k, piece in enumerate(pieces):
                    extra = jnp.where(index == k, piece, extra)
                out[6 * dim :, lanes] = extra.astype(jnp.bfloat16)

        def fill(dst, lhs, rhs, major, minor):
            def one_row(rb, carry):
                rows = pl.ds(pl.multiple_of(rb * TILE, TILE), TILE)
                block = lhs[:, rows]
                for cb in range(tiles):
                    product = lax.dot_general(
                        block,
                        rhs[:, cb * TILE : (cb + 1) * TILE],
                        (((0,), (0,)), ((), ())),
                        preferred_element_type=jnp.float32,
                    )
                    tile = rb * major + cb * minor
                    extra = penalty[pl.ds(pl.multiple_of(tile * 8, 8), 8), :]
                    dst[rows, cb * TILE : (cb + 1) * TILE] = product + jnp.broadcast_to(
                        extra[0:1, 0:1], product.shape
                    )
                return carry

            lax.fori_loop(0, tiles, one_row, 0)

        def local_lse(costs, potential):
            turned = potential.T
            for b in range(blocks):
                spread[b * LANES : (b + 1) * LANES, :] = jnp.broadcast_to(
                    turned[:, b : b + 1], (LANES, LANES)
                )

            def step(g, carry):
                rows = pl.ds(pl.multiple_of(g * SPAN, SPAN), SPAN)
                shift = spread[rows, :]
                result = []
                for b in range(blocks):
                    highest, total = carry[b]
                    scores = shift - costs[rows, b * LANES : (b + 1) * LANES]
                    scores = scores.reshape(SPAN // 8, 8, LANES)
                    raised = jnp.maximum(highest, jnp.max(scores, axis=0))
                    fresh = jnp.sum(jnp.exp2(scores - raised[None]), axis=0)
                    result.append((raised, total * jnp.exp2(highest - raised) + fresh))
                return tuple(result)

            low = jnp.full((8, LANES), -3e38, jnp.float32)
            none = jnp.zeros((8, LANES), jnp.float32)
            pairs = lax.fori_loop(
                0, cells // SPAN, step, tuple((low, none) for b in range(blocks)), unroll=UNROLL
            )
            index = lax.broadcasted_iota(jnp.int32, (blocks, LANES), 0)
            lse_max = jnp.zeros((blocks, LANES), jnp.float32)
            lse_sum = jnp.ones((blocks, LANES), jnp.float32)
            for b in range(blocks):
                highest, total = pairs[b]
                top = jnp.max(highest, axis=0, keepdims=True)
                total = jnp.sum(total * jnp.exp2(highest - top), axis=0, keepdims=True)
                lse_max = jnp.where(index == b, top, lse_max)
                lse_sum = jnp.where(index == b, total, lse_sum)
            return lse_max + jnp.log2(lse_sum)

        y_order = sorted(range(len(y_offsets)), key=lambda k: -k)
        z_order = sorted(range(len(chain_offsets)), key=lambda k: -k)
        for i in range(max(len(y_order), len(z_order))):
            if i < len(y_order):
                k = y_order[i]
                chunk = src_chunk(x * ring_y + (y + ring_y - y_offsets[k]) % ring_y)
                wait_bytes(chunk, y_recv.at[k])
                for peer in x_peers:
                    send(chunk, chunk, gather_send.at[2], x_recv, peer)
            if i < len(z_order):
                k = z_order[i]
                chunk = tgt_chunk((z + ring_z - chain_offsets[k]) % ring_z * CORES + core)
                wait_bytes(chunk, z_recv.at[k])
                send(chunk, chunk, gather_send.at[3], pair_recv, partner)

        wait_bytes(gtgt.at[pl.ds(0, ring_z * tgt_size)], pair_recv)
        operands(gtgt, right, tgt_rows, 1.0, False)
        wait_bytes(gsrc.at[pl.ds(0, len(x_peers) * ring_y * src_size)], x_recv)
        operands(gsrc, left, src_rows, -2.0 * unit, True)
        fill(cost_t, right, left, 1, tiles)

        source_mass = smass_ref[...] * log2e
        target_mass = tmass_ref[...] * log2e

        def iterate(turn, carry):
            target_side = carry[1]
            part_row[turn] = local_lse(cost_t, target_side)
            for k, peer in enumerate(plane_peers):
                send(part_row.at[turn], got_row.at[turn, k], row_send, row_recv.at[turn], peer)

            @pl.when(turn == 0)
            def fill_cost():
                fill(cost, left, right, tiles, 1)

            wait_bytes(got_row.at[turn], row_recv.at[turn])
            lse = combine([part_row[turn]] + [got_row[turn, k] for k in range(len(plane_peers))])
            source_side = source_mass - lse

            part_col[turn] = local_lse(cost, source_side)
            for k, peer in enumerate(z_peers):
                send(part_col.at[turn], got_col.at[turn, k], col_send, col_recv.at[turn], peer)
            wait_bytes(got_col.at[turn], col_recv.at[turn])
            lse = combine([part_col[turn]] + [got_col[turn, k] for k in range(len(z_peers))])
            return source_side, target_mass - lse

        zero = jnp.zeros((blocks, LANES), jnp.float32)
        source_side, target_side = lax.fori_loop(0, ITERS, iterate, (zero, zero))
        source_out[...] = source_side
        target_out[...] = target_side

        wait_bytes(gsrc.at[pl.ds(0, len(y_peers) * src_size)], gather_send.at[0])
        wait_bytes(gtgt.at[pl.ds(0, len(chain_peers) * tgt_size)], gather_send.at[1])
        wait_bytes(gsrc.at[pl.ds(0, len(x_peers) * ring_y * src_size)], gather_send.at[2])
        wait_bytes(gtgt.at[pl.ds(0, ring_z * tgt_size)], gather_send.at[3])
        wait_bytes(got_row, row_send)
        wait_bytes(got_col, col_send)

    def vector(count):
        return pltpu.VMEM((ITERS, count, blocks, LANES), jnp.float32)

    depth = 6 * dim + LANES
    scratch = [
        pltpu.VMEM((src_rows, cells), jnp.float32),
        pltpu.VMEM((tgt_rows, cells), jnp.float32),
        pltpu.VMEM((blocks, LANES), jnp.float32),
        pltpu.VMEM((blocks, LANES), jnp.float32),
        pltpu.VMEM((1, 1, 2, slot_count), jnp.int32),
        pltpu.VMEM((1, 1), jnp.int32),
        pltpu.VMEM((dim * blocks, LANES), jnp.float32),
        pltpu.VMEM((dim * blocks, LANES), jnp.float32),
        pltpu.VMEM((depth, cells), jnp.bfloat16),
        pltpu.VMEM((depth, cells), jnp.bfloat16),
        pltpu.VMEM((cells, cells), jnp.float32),
        pltpu.VMEM((cells, cells), jnp.float32),
        pltpu.VMEM((tiles * tiles * 8, LANES), jnp.float32),
        pltpu.VMEM((cells, LANES), jnp.float32),
        pltpu.VMEM((ITERS, blocks, LANES), jnp.float32),
        pltpu.VMEM((ITERS, blocks, LANES), jnp.float32),
        vector(len(plane_offsets)),
        vector(len(z_offsets)),
        pltpu.SemaphoreType.DMA((6,)),
        pltpu.SemaphoreType.DMA((4,)),
        pltpu.SemaphoreType.DMA((len(y_offsets),)),
        pltpu.SemaphoreType.DMA((len(chain_offsets),)),
        pltpu.SemaphoreType.DMA,
        pltpu.SemaphoreType.DMA,
        pltpu.SemaphoreType.DMA,
        pltpu.SemaphoreType.DMA,
        pltpu.SemaphoreType.DMA((ITERS,)),
        pltpu.SemaphoreType.DMA((ITERS,)),
    ]
    return kernel, scratch


def shards(n_row, n_col, source_embed, target_embed, source_mass, target_mass, tile_list, tile_counts):
    cells = source_embed.shape[1]
    dim = source_embed.shape[0] * n_col
    blocks = cells // LANES
    kernel, scratch = make_kernel(n_row, n_col, RING_Y, cells, dim, tile_list.shape[3])
    side = jax.ShapeDtypeStruct((blocks, LANES), jnp.float32)
    source_side, target_side = pl.pallas_call(
        kernel,
        out_shape=(side, side),
        in_specs=[pl.BlockSpec(memory_space=pl.ANY)] * 6,
        out_specs=[pl.BlockSpec(memory_space=pltpu.VMEM)] * 2,
        scratch_shapes=scratch,
        compiler_params=pltpu.CompilerParams(collective_id=0, has_side_effects=True),
        name="sinkhorn",
    )(
        source_embed,
        target_embed,
        source_mass.reshape(blocks, LANES),
        target_mass.reshape(blocks, LANES),
        tile_list,
        tile_counts,
    )
    unit = entropic / log2e
    return (source_side * unit).reshape(cells), (target_side * unit).reshape(cells)


def solution(mesh):
    in_specs = (
        P("col", "row"),
        P("row", "col"),
        P("row"),
        P("col"),
        P("row", "col", None, None),
        P("row", "col"),
    )
    out_specs = (P("row"), P("col"))
    body = functools.partial(shards, mesh.shape["row"], mesh.shape["col"])
    return jax.shard_map(body, mesh=mesh, in_specs=in_specs, out_specs=out_specs, check_vma=False)
```

time: 80.2 us -> 71.6 us (0.89)
  Pallas kernels: 77.3 us -> 68.9 us
    pallas_call x1, Pallas kernels: 77.3 us -> 68.9 us  [shards(): pl.pallas_call(kernel, out_shape=(side, side), in_specs=[pl.BlockSpec(mem...]
    reshape x0 -> x1, other arithmetic: none -> 1.28 us  [shards(): (target_side * unit).reshape(cells)]
where the time goes in v2:
time: 71.6 us; the launch traced here: 71.4 us
  Pallas kernels  68.9 us (96%)
  between operations  1.29 us (2%)
  other arithmetic  1.28 us (2%)
    pallas_call x1, Pallas kernels, shards(): pl.pallas_call(kernel, out_shape=(side, side), in_specs=[pl.BlockSpec(mem...  68.9 us

profile of v2, /device:TPU:1, one launch (start us, length us, event | category | flops | bytes accessed | tf_op | source)
XLA Modules:
  0.0 71.4 jit_solution(10738401356321400785)
XLA Ops:
  1.3 68.9 %sinkhorn.1 = (f32[8,128]{1,0:T(8,128)}, f32[8,128]{1,0:T(8,128)}) custom-call(f32[2,1024]{1,0:T(2,128)} %src_hbm.1, f32[4,1024]{1,0:T(4,128)} %tgt_hbm.1, f32[8,128]{1,0:T(8,128)} %bitcast.6, f32[8,128]{1,0:T(8,128)} %bitcast.7, s32[1,1,2,12]{3,2,1,0:T(2,128)} %list_hbm.1, s32[1,1]{1,0:T(1,128)S(6)} %copy.8.count_hbm), custom_call_target="tpu_custom_call" | custom-call | tf_op jit(solution)/shard_map/sinkhorn/pallas_call | solution.py:372
  70.1 1.3 %multiply_bitcast_fusion = (f32[1024]{0:T(1024)}, f32[1024]{0:T(1024)}) fusion(f32[8,128]{1,0:T(8,128)} %get-tuple-element.5, f32[8,128]{1,0:T(8,128)} %get-tuple-element.4), kind=kLoop, calls=%fused_computation | loop fusion | flops 2048 | bytes 16384 | tf_op jit(solution)/shard_map/reshape | solution.py:389

commit v3 on v2

--- a/solution.py
+++ b/solution.py
@@ -14,16 +14,13 @@
 CORES = 2
 SPAN = 64
 UNROLL = 4
+HALVES = 2
 
 entropic = 0.1
 dead_cost = 1e30
 log2e = math.log2(math.e)
 MESH = pl.DeviceIdType.MESH
 LANES = 128
-
-
-def blocks_of(cells):
-    return cells // LANES
 
 
 def ring_offsets(size):
@@ -51,13 +48,14 @@
 def make_kernel(n_row, n_col, ring_y, cells, dim, slot_count):
     ring_x = n_col // ring_y
     ring_z = n_row // CORES
-    blocks = blocks_of(cells)
+    blocks = cells // LANES
     src_rows = dim // n_col
     tgt_rows = dim // n_row
     per = max(src_rows, tgt_rows)
     steps = dim // per
-    src_size = src_rows * blocks_of(cells)
-    tgt_size = tgt_rows * blocks_of(cells)
+    part = blocks // HALVES
+    src_size = src_rows * blocks
+    tgt_size = tgt_rows * blocks
     tiles = cells // TILE
     x_offsets = ring_offsets(ring_x)
     y_offsets = ring_offsets(ring_y)
@@ -90,6 +88,7 @@
         cost_t,
         penalty,
         spread,
+        state,
         part_row,
         part_col,
         got_row,
@@ -233,19 +232,22 @@
 
             lax.fori_loop(0, tiles, one_row, 0)
 
-        def local_lse(costs, potential):
+        def spread_half(potential, half):
             turned = potential.T
-            for b in range(blocks):
-                spread[b * LANES : (b + 1) * LANES, :] = jnp.broadcast_to(
+            for b in range(part):
+                start = (half * part + b) * LANES
+                spread[start : start + LANES, :] = jnp.broadcast_to(
                     turned[:, b : b + 1], (LANES, LANES)
                 )
 
+        def sweep(costs, half, chosen, pairs):
+            reach = cells // HALVES
+
             def step(g, carry):
-                rows = pl.ds(pl.multiple_of(g * SPAN, SPAN), SPAN)
+                rows = pl.ds(pl.multiple_of(half * reach + g * SPAN, SPAN), SPAN)
                 shift = spread[rows, :]
                 result = []
-                for b in range(blocks):
-                    highest, total = carry[b]
+                for b, (highest, total) in zip(chosen, carry):
                     scores = shift - costs[rows, b * LANES : (b + 1) * LANES]
                     scores = scores.reshape(SPAN // 8, 8, LANES)
                     raised = jnp.maximum(highest, jnp.max(scores, axis=0))
@@ -253,21 +255,37 @@
                     result.append((raised, total * jnp.exp2(highest - raised) + fresh))
                 return tuple(result)
 
-            low = jnp.full((8, LANES), -3e38, jnp.float32)
-            none = jnp.zeros((8, LANES), jnp.float32)
-            pairs = lax.fori_loop(
-                0, cells // SPAN, step, tuple((low, none) for b in range(blocks)), unroll=UNROLL
-            )
-            index = lax.broadcasted_iota(jnp.int32, (blocks, LANES), 0)
-            lse_max = jnp.zeros((blocks, LANES), jnp.float32)
-            lse_sum = jnp.ones((blocks, LANES), jnp.float32)
-            for b in range(blocks):
-                highest, total = pairs[b]
+            return lax.fori_loop(0, reach // SPAN, step, tuple(pairs), unroll=UNROLL)
+
+        def finish(pairs):
+            index = lax.broadcasted_iota(jnp.int32, (part, LANES), 0)
+            lse_max = jnp.zeros((part, LANES), jnp.float32)
+            lse_sum = jnp.ones((part, LANES), jnp.float32)
+            for b, (highest, total) in enumerate(pairs):
                 top = jnp.max(highest, axis=0, keepdims=True)
                 total = jnp.sum(total * jnp.exp2(highest - top), axis=0, keepdims=True)
                 lse_max = jnp.where(index == b, top, lse_max)
                 lse_sum = jnp.where(index == b, total, lse_sum)
             return lse_max + jnp.log2(lse_sum)
+
+        def open_pass(costs, potential):
+            spread_half(potential, 0)
+            low = jnp.full((8, LANES), -3e38, jnp.float32)
+            none = jnp.zeros((8, LANES), jnp.float32)
+            pairs = sweep(costs, 0, range(blocks), [(low, none)] * blocks)
+            for b, (highest, total) in enumerate(pairs):
+                state[0, b] = highest
+                state[1, b] = total
+
+        def close_pass(costs, potential, emit):
+            spread_half(potential, 1)
+            for half in range(HALVES):
+                chosen = range(half * part, (half + 1) * part)
+                pairs = sweep(costs, 1, chosen, [(state[0, b], state[1, b]) for b in chosen])
+                emit(half, finish(pairs))
+
+        def merged(own, got, turn, half, count):
+            return combine([own[turn, half]] + [got[turn, half, k] for k in range(count)])
 
         y_order = sorted(range(len(y_offsets)), key=lambda k: -k)
         z_order = sorted(range(len(chain_offsets)), key=lambda k: -k)
@@ -290,34 +308,63 @@
         operands(gsrc, left, src_rows, -2.0 * unit, True)
         fill(cost_t, right, left, 1, tiles)
 
-        source_mass = smass_ref[...] * log2e
-        target_mass = tmass_ref[...] * log2e
-
-        def iterate(turn, carry):
-            target_side = carry[1]
-            part_row[turn] = local_lse(cost_t, target_side)
-            for k, peer in enumerate(plane_peers):
-                send(part_row.at[turn], got_row.at[turn, k], row_send, row_recv.at[turn], peer)
+        source_mass = [smass_ref[h * part : (h + 1) * part, :] * log2e for h in range(HALVES)]
+        target_mass = [tmass_ref[h * part : (h + 1) * part, :] * log2e for h in range(HALVES)]
+        zero = jnp.zeros((part, LANES), jnp.float32)
+        open_pass(cost_t, zero)
+
+        def iterate(turn, target_late):
+            def emit_row(half, lse):
+                part_row[turn, half] = lse
+                for k, peer in enumerate(plane_peers):
+                    send(
+                        part_row.at[turn, half],
+                        got_row.at[turn, half, k],
+                        row_send,
+                        row_recv.at[turn, half],
+                        peer,
+                    )
+
+            def emit_col(half, lse):
+                part_col[turn, half] = lse
+                for k, peer in enumerate(z_peers):
+                    send(
+                        part_col.at[turn, half],
+                        got_col.at[turn, half, k],
+                        col_send,
+                        col_recv.at[turn, half],
+                        peer,
+                    )
+
+            def source_half(half):
+                wait_bytes(got_row.at[turn, half], row_recv.at[turn, half])
+                lse = merged(part_row, got_row, turn, half, len(plane_peers))
+                source_out[half * part : (half + 1) * part, :] = source_mass[half] - lse
+                return source_mass[half] - lse
+
+            def target_half(half):
+                wait_bytes(got_col.at[turn, half], col_recv.at[turn, half])
+                lse = merged(part_col, got_col, turn, half, len(z_peers))
+                target_out[half * part : (half + 1) * part, :] = target_mass[half] - lse
+                return target_mass[half] - lse
+
+            close_pass(cost_t, target_late, emit_row)
 
             @pl.when(turn == 0)
             def fill_cost():
                 fill(cost, left, right, tiles, 1)
 
-            wait_bytes(got_row.at[turn], row_recv.at[turn])
-            lse = combine([part_row[turn]] + [got_row[turn, k] for k in range(len(plane_peers))])
-            source_side = source_mass - lse
-
-            part_col[turn] = local_lse(cost, source_side)
-            for k, peer in enumerate(z_peers):
-                send(part_col.at[turn], got_col.at[turn, k], col_send, col_recv.at[turn], peer)
-            wait_bytes(got_col.at[turn], col_recv.at[turn])
-            lse = combine([part_col[turn]] + [got_col[turn, k] for k in range(len(z_peers))])
-            return source_side, target_mass - lse
-
-        zero = jnp.zeros((blocks, LANES), jnp.float32)
-        source_side, target_side = lax.fori_loop(0, ITERS, iterate, (zero, zero))
-        source_out[...] = source_side
-        target_out[...] = target_side
+            open_pass(cost, source_half(0))
+            close_pass(cost, source_half(1), emit_col)
+            target_early = target_half(0)
+
+            @pl.when(turn < ITERS - 1)
+            def next_pass():
+                open_pass(cost_t, target_early)
+
+            return target_half(1)
+
+        lax.fori_loop(0, ITERS, iterate, zero)
 
         wait_bytes(gsrc.at[pl.ds(0, len(y_peers) * src_size)], gather_send.at[0])
         wait_bytes(gtgt.at[pl.ds(0, len(chain_peers) * tgt_size)], gather_send.at[1])
@@ -327,7 +374,7 @@
         wait_bytes(got_col, col_send)
 
     def vector(count):
-        return pltpu.VMEM((ITERS, count, blocks, LANES), jnp.float32)
+        return pltpu.VMEM((ITERS, HALVES, count, part, LANES), jnp.float32)
 
     depth = 6 * dim + LANES
     scratch = [
@@ -345,8 +392,9 @@
         pltpu.VMEM((cells, cells), jnp.float32),
         pltpu.VMEM((tiles * tiles * 8, LANES), jnp.float32),
         pltpu.VMEM((cells, LANES), jnp.float32),
-        pltpu.VMEM((ITERS, blocks, LANES), jnp.float32),
-        pltpu.VMEM((ITERS, blocks, LANES), jnp.float32),
+        pltpu.VMEM((2, blocks, 8, LANES), jnp.float32),
+        pltpu.VMEM((ITERS, HALVES, part, LANES), jnp.float32),
+        pltpu.VMEM((ITERS, HALVES, part, LANES), jnp.float32),
         vector(len(plane_offsets)),
         vector(len(z_offsets)),
         pltpu.SemaphoreType.DMA((6,)),
@@ -357,8 +405,8 @@
         pltpu.SemaphoreType.DMA,
         pltpu.SemaphoreType.DMA,
         pltpu.SemaphoreType.DMA,
-        pltpu.SemaphoreType.DMA((ITERS,)),
-        pltpu.SemaphoreType.DMA((ITERS,)),
+        pltpu.SemaphoreType.DMA((ITERS, HALVES)),
+        pltpu.SemaphoreType.DMA((ITERS, HALVES)),
     ]
     return kernel, scratch
 
@@ -368,7 +416,7 @@
     dim = source_embed.shape[0] * n_col
     blocks = cells // LANES
     kernel, scratch = make_kernel(n_row, n_col, RING_Y, cells, dim, tile_list.shape[3])
-    side = jax.ShapeDtypeStruct((blocks, LANES), jnp.float32)
+    side = pltpu.VMEM((blocks, LANES), jnp.float32)
     source_side, target_side = pl.pallas_call(
         kernel,
         out_shape=(side, side),

time: 71.6 us -> 70.1 us (0.979)
  Pallas kernels: 68.9 us -> 68 us
    pallas_call x1, Pallas kernels: 68.9 us -> 68 us  [shards(): pl.pallas_call(kernel, out_shape=(side, side), in_specs=[pl.BlockSpec(mem...]
where the time goes in v3:
time: 70.1 us; the launch traced here: 69.9 us
  Pallas kernels  68 us (97%)
  between operations  1.29 us (2%)
    pallas_call x1, Pallas kernels, shards(): pl.pallas_call(kernel, out_shape=(side, side), in_specs=[pl.BlockSpec(mem...  68 us

profile of v3, /device:TPU:1, one launch (start us, length us, event | category | flops | bytes accessed | tf_op | source)
XLA Modules:
  0.0 69.9 jit_solution(4469884803571948608)
XLA Ops:
  1.3 68.0 %sinkhorn.1 = (f32[8,128]{1,0:T(8,128)S(1)}, f32[8,128]{1,0:T(8,128)S(1)}) custom-call(f32[2,1024]{1,0:T(2,128)} %src_hbm.1, f32[4,1024]{1,0:T(4,128)} %tgt_hbm.1, f32[8,128]{1,0:T(8,128)} %bitcast.6, f32[8,128]{1,0:T(8,128)} %bitcast.7, s32[1,1,2,12]{3,2,1,0:T(2,128)} %list_hbm.1, s32[1,1]{1,0:T(1,128)S(6)} %copy.8.count_hbm), custom_call_target="tpu_custom_call" | custom-call | tf_op jit(solution)/shard_map/sinkhorn/pallas_call | solution.py:420
  69.3 0.6 multiply_bitcast_fusion

commit v4 on v3

--- a/solution.py
+++ b/solution.py
@@ -62,8 +62,15 @@
     z_offsets = [(0, 1)] + [(dz, dc) for dz in range(1, ring_z) for dc in range(CORES)]
     z_offsets.sort(key=lambda o: -min(o[0], ring_z - o[0]))
     chain_offsets = ring_offsets(ring_z)
+    def reach_of(dx, dy):
+        return min(dx, ring_x - dx) + min(dy, ring_y - dy)
+
     plane_offsets = [(dx, dy) for dx in range(ring_x) for dy in range(ring_y) if dx or dy]
-    plane_offsets.sort(key=lambda o: -min(o[0], ring_x - o[0]) - min(o[1], ring_y - o[1]))
+    plane_offsets.sort(key=lambda o: -reach_of(*o))
+    plane_far = sum(2 * reach_of(*o) > ring_x // 2 + ring_y // 2 for o in plane_offsets)
+    plane_near = len(plane_offsets) - plane_far
+    z_far = sum(2 * min(dz, ring_z - dz) > ring_z // 2 for dz, dc in z_offsets)
+    z_near = len(z_offsets) - z_far
 
     def kernel(
         src_hbm,
@@ -91,8 +98,10 @@
         state,
         part_row,
         part_col,
-        got_row,
-        got_col,
+        far_row,
+        far_col,
+        near_row,
+        near_col,
         load_sem,
         gather_send,
         y_recv,
@@ -101,8 +110,10 @@
         pair_recv,
         row_send,
         col_send,
-        row_recv,
-        col_recv,
+        far_row_recv,
+        far_col_recv,
+        near_row_recv,
+        near_col_recv,
     ):
         row = lax.axis_index("row")
         col = lax.axis_index("col")
@@ -284,23 +295,38 @@
                 pairs = sweep(costs, 1, chosen, [(state[0, b], state[1, b]) for b in chosen])
                 emit(half, finish(pairs))
 
-        def merged(own, got, turn, half, count):
-            return combine([own[turn, half]] + [got[turn, half, k] for k in range(count)])
-
-        y_order = sorted(range(len(y_offsets)), key=lambda k: -k)
-        z_order = sorted(range(len(chain_offsets)), key=lambda k: -k)
-        for i in range(max(len(y_order), len(z_order))):
-            if i < len(y_order):
-                k = y_order[i]
+        def merged(own, far, near, turn, half):
+            parts = [far[turn, half, k] for k in range(far.shape[2])]
+            parts += [near[turn, k, half] for k in range(near.shape[1])]
+            return combine([own[turn, half]] + parts)
+
+        def emit_to(peers, own, far, near, sends, far_recv, near_recv, turn, half, lse):
+            own[turn, half] = lse
+            far_count = far.shape[2]
+            for k, peer in enumerate(peers[:far_count]):
+                send(
+                    own.at[turn, half],
+                    far.at[turn, half, k],
+                    sends.at[0],
+                    far_recv.at[turn, half],
+                    peer,
+                )
+            if half == HALVES - 1:
+                for k, peer in enumerate(peers[far_count:]):
+                    send(own.at[turn], near.at[turn, k], sends.at[1], near_recv.at[turn], peer)
+
+        arrivals = [(min(d, ring_y - d), 0, k) for k, d in enumerate(y_offsets)]
+        arrivals += [(min(d, ring_z - d) + 1.5, 1, k) for k, d in enumerate(chain_offsets)]
+        for when, chain, k in sorted(arrivals):
+            if chain:
+                chunk = tgt_chunk((z + ring_z - chain_offsets[k]) % ring_z * CORES + core)
+                wait_bytes(chunk, z_recv.at[k])
+                send(chunk, chunk, gather_send.at[3], pair_recv, partner)
+            else:
                 chunk = src_chunk(x * ring_y + (y + ring_y - y_offsets[k]) % ring_y)
                 wait_bytes(chunk, y_recv.at[k])
                 for peer in x_peers:
                     send(chunk, chunk, gather_send.at[2], x_recv, peer)
-            if i < len(z_order):
-                k = z_order[i]
-                chunk = tgt_chunk((z + ring_z - chain_offsets[k]) % ring_z * CORES + core)
-                wait_bytes(chunk, z_recv.at[k])
-                send(chunk, chunk, gather_send.at[3], pair_recv, partner)
 
         wait_bytes(gtgt.at[pl.ds(0, ring_z * tgt_size)], pair_recv)
         operands(gtgt, right, tgt_rows, 1.0, False)
@@ -314,37 +340,42 @@
         open_pass(cost_t, zero)
 
         def iterate(turn, target_late):
-            def emit_row(half, lse):
-                part_row[turn, half] = lse
-                for k, peer in enumerate(plane_peers):
-                    send(
-                        part_row.at[turn, half],
-                        got_row.at[turn, half, k],
-                        row_send,
-                        row_recv.at[turn, half],
-                        peer,
-                    )
-
-            def emit_col(half, lse):
-                part_col[turn, half] = lse
-                for k, peer in enumerate(z_peers):
-                    send(
-                        part_col.at[turn, half],
-                        got_col.at[turn, half, k],
-                        col_send,
-                        col_recv.at[turn, half],
-                        peer,
-                    )
+            emit_row = functools.partial(
+                emit_to,
+                plane_peers,
+                part_row,
+                far_row,
+                near_row,
+                row_send,
+                far_row_recv,
+                near_row_recv,
+                turn,
+            )
+            emit_col = functools.partial(
+                emit_to,
+                z_peers,
+                part_col,
+                far_col,
+                near_col,
+                col_send,
+                far_col_recv,
+                near_col_recv,
+                turn,
+            )
 
             def source_half(half):
-                wait_bytes(got_row.at[turn, half], row_recv.at[turn, half])
-                lse = merged(part_row, got_row, turn, half, len(plane_peers))
+                wait_bytes(far_row.at[turn, half], far_row_recv.at[turn, half])
+                if half == 0:
+                    wait_bytes(near_row.at[turn], near_row_recv.at[turn])
+                lse = merged(part_row, far_row, near_row, turn, half)
                 source_out[half * part : (half + 1) * part, :] = source_mass[half] - lse
                 return source_mass[half] - lse
 
             def target_half(half):
-                wait_bytes(got_col.at[turn, half], col_recv.at[turn, half])
-                lse = merged(part_col, got_col, turn, half, len(z_peers))
+                wait_bytes(far_col.at[turn, half], far_col_recv.at[turn, half])
+                if half == 0:
+                    wait_bytes(near_col.at[turn], near_col_recv.at[turn])
+                lse = merged(part_col, far_col, near_col, turn, half)
                 target_out[half * part : (half + 1) * part, :] = target_mass[half] - lse
                 return target_mass[half] - lse
 
@@ -370,11 +401,16 @@
         wait_bytes(gtgt.at[pl.ds(0, len(chain_peers) * tgt_size)], gather_send.at[1])
         wait_bytes(gsrc.at[pl.ds(0, len(x_peers) * ring_y * src_size)], gather_send.at[2])
         wait_bytes(gtgt.at[pl.ds(0, ring_z * tgt_size)], gather_send.at[3])
-        wait_bytes(got_row, row_send)
-        wait_bytes(got_col, col_send)
-
-    def vector(count):
+        wait_bytes(far_row, row_send.at[0])
+        wait_bytes(near_row, row_send.at[1])
+        wait_bytes(far_col, col_send.at[0])
+        wait_bytes(near_col, col_send.at[1])
+
+    def far_slots(count):
         return pltpu.VMEM((ITERS, HALVES, count, part, LANES), jnp.float32)
+
+    def near_slots(count):
+        return pltpu.VMEM((ITERS, count, HALVES, part, LANES), jnp.float32)
 
     depth = 6 * dim + LANES
     scratch = [
@@ -395,18 +431,22 @@
         pltpu.VMEM((2, blocks, 8, LANES), jnp.float32),
         pltpu.VMEM((ITERS, HALVES, part, LANES), jnp.float32),
         pltpu.VMEM((ITERS, HALVES, part, LANES), jnp.float32),
-        vector(len(plane_offsets)),
-        vector(len(z_offsets)),
+        far_slots(plane_far),
+        far_slots(z_far),
+        near_slots(plane_near),
+        near_slots(z_near),
         pltpu.SemaphoreType.DMA((6,)),
         pltpu.SemaphoreType.DMA((4,)),
         pltpu.SemaphoreType.DMA((len(y_offsets),)),
         pltpu.SemaphoreType.DMA((len(chain_offsets),)),
         pltpu.SemaphoreType.DMA,
         pltpu.SemaphoreType.DMA,
-        pltpu.SemaphoreType.DMA,
-        pltpu.SemaphoreType.DMA,
+        pltpu.SemaphoreType.DMA((2,)),
+        pltpu.SemaphoreType.DMA((2,)),
         pltpu.SemaphoreType.DMA((ITERS, HALVES)),
         pltpu.SemaphoreType.DMA((ITERS, HALVES)),
+        pltpu.SemaphoreType.DMA((ITERS,)),
+        pltpu.SemaphoreType.DMA((ITERS,)),
     ]
     return kernel, scratch
 

time: 70.1 us -> 70.2 us (level)
  no operation moved by 1% of the time
where the time goes in v4:
time: 70.2 us; the launch traced here: 70 us
  Pallas kernels  68.1 us (97%)
  between operations  1.29 us (2%)
    pallas_call x1, Pallas kernels, shards(): pl.pallas_call(kernel, out_shape=(side, side), in_specs=[pl.BlockSpec(mem...  68.1 us

profile of v4, /device:TPU:1, one launch (start us, length us, event | category | flops | bytes accessed | tf_op | source)
XLA Modules:
  0.0 70.0 jit_solution(17187651521909169432)
XLA Ops:
  1.3 68.1 %sinkhorn.1 = (f32[8,128]{1,0:T(8,128)S(1)}, f32[8,128]{1,0:T(8,128)S(1)}) custom-call(f32[2,1024]{1,0:T(2,128)} %src_hbm.1, f32[4,1024]{1,0:T(4,128)} %tgt_hbm.1, f32[8,128]{1,0:T(8,128)} %bitcast.6, f32[8,128]{1,0:T(8,128)} %bitcast.7, s32[1,1,2,12]{3,2,1,0:T(2,128)} %list_hbm.1, s32[1,1]{1,0:T(1,128)S(6)} %copy.8.count_hbm), custom_call_target="tpu_custom_call" | custom-call | tf_op jit(solution)/shard_map/sinkhorn/pallas_call | solution.py:460
  69.4 0.6 multiply_bitcast_fusion

commit v5 on v4

--- a/solution.py
+++ b/solution.py
@@ -21,10 +21,6 @@
 log2e = math.log2(math.e)
 MESH = pl.DeviceIdType.MESH
 LANES = 128
-
-
-def ring_offsets(size):
-    return sorted(range(1, size), key=lambda k: -min(k, size - k))
 
 
 def wait_bytes(ref, sem):
@@ -57,11 +53,9 @@
     src_size = src_rows * blocks
     tgt_size = tgt_rows * blocks
     tiles = cells // TILE
-    x_offsets = ring_offsets(ring_x)
-    y_offsets = ring_offsets(ring_y)
+    rest_chunks = (ring_x - 1) * ring_y - (ring_y if ring_x > 3 else 0)
     z_offsets = [(0, 1)] + [(dz, dc) for dz in range(1, ring_z) for dc in range(CORES)]
     z_offsets.sort(key=lambda o: -min(o[0], ring_z - o[0]))
-    chain_offsets = ring_offsets(ring_z)
     def reach_of(dx, dy):
         return min(dx, ring_x - dx) + min(dy, ring_y - dy)
 
@@ -107,6 +101,7 @@
         y_recv,
         z_recv,
         x_recv,
+        x_relay,
         pair_recv,
         row_send,
         col_send,
@@ -119,9 +114,18 @@
         col = lax.axis_index("col")
         x, y = col // ring_y, col % ring_y
         z, core = row // CORES, row % CORES
-        x_peers = [(row, (x + dx) % ring_x * ring_y + y) for dx in x_offsets]
-        y_peers = [(row, x * ring_y + (y + dy) % ring_y) for dy in y_offsets]
-        chain_peers = [((z + dz) % ring_z * CORES + core, col) for dz in chain_offsets]
+        def x_step(dx):
+            return (row, (x + dx + ring_x) % ring_x * ring_y + y)
+
+        def y_step(dy):
+            return (row, x * ring_y + (y + dy + ring_y) % ring_y)
+
+        def z_step(dz):
+            return ((z + dz + ring_z) % ring_z * CORES + core, col)
+
+        def beside(step, size):
+            return [step(1), step(-1)] if size > 2 else [step(1)] if size > 1 else []
+
         partner = (z * CORES + (core + 1) % CORES, col)
         z_peers = [((z + dz) % ring_z * CORES + (core + dc) % CORES, col) for dz, dc in z_offsets]
         plane_peers = [
@@ -144,7 +148,7 @@
         for load in loads:
             load.start()
         barrier = pltpu.get_barrier_semaphore()
-        greeted = y_peers + z_peers + x_peers
+        greeted = [partner] + beside(y_step, ring_y) + beside(z_step, ring_z) + beside(x_step, ring_x)
         for peer in greeted:
             pl.semaphore_signal(barrier, inc=1, device_id=peer, device_id_type=MESH)
 
@@ -174,12 +178,23 @@
                 device_id_type=MESH,
             ).start()
 
-        for k, peer in enumerate(y_peers):
-            send(own_src, own_src, gather_send.at[0], y_recv.at[k], peer)
-        for k, peer in enumerate(chain_peers):
-            send(own_tgt, own_tgt, gather_send.at[1], z_recv.at[k], peer)
-        for peer in x_peers:
-            send(own_src, own_src, gather_send.at[2], x_recv, peer)
+        def pass_on(chunk, step, size, distance, send_sem, recv):
+            for way in (1, -1) if distance == 0 else (1 if distance > 0 else -1,):
+                after = abs(distance) + 1
+                limit = size // 2 if way > 0 else (size - 1) // 2
+                if after <= limit:
+                    slot = after - 1 if way > 0 else size // 2 + after - 1
+                    send(chunk, chunk, send_sem, recv.at[slot], step(way))
+
+        def hand_out(chunk, q):
+            for way in (1, -1)[: min(ring_x - 1, 2)]:
+                relayed = ring_x > 3 and (way > 0) == (q % 2 == 0)
+                recv = x_relay.at[q] if relayed else x_recv
+                send(chunk, chunk, gather_send.at[2], recv, x_step(way))
+
+        pass_on(own_src, y_step, ring_y, 0, gather_send.at[0], y_recv)
+        pass_on(own_tgt, z_step, ring_z, 0, gather_send.at[1], z_recv)
+        hand_out(own_src, 0)
         send(own_tgt, own_tgt, gather_send.at[3], pair_recv, partner)
 
         slots = list_ref[0, 0]
@@ -315,22 +330,35 @@
                 for k, peer in enumerate(peers[far_count:]):
                     send(own.at[turn], near.at[turn, k], sends.at[1], near_recv.at[turn], peer)
 
-        arrivals = [(min(d, ring_y - d), 0, k) for k, d in enumerate(y_offsets)]
-        arrivals += [(min(d, ring_z - d) + 1.5, 1, k) for k, d in enumerate(chain_offsets)]
-        for when, chain, k in sorted(arrivals):
-            if chain:
-                chunk = tgt_chunk((z + ring_z - chain_offsets[k]) % ring_z * CORES + core)
-                wait_bytes(chunk, z_recv.at[k])
+        events = []
+        for size, kind in ((ring_y, 0), (ring_z, 1)):
+            for d in range(1, size // 2 + 1):
+                events.append((1.7 * d + 0.2 * kind, kind, d, d - 1))
+            for d in range(1, (size - 1) // 2 + 1):
+                events.append((1.7 * d + 0.2 * kind, kind, -d, size // 2 + d - 1))
+        for q in range(ring_y if ring_x > 3 else 0):
+            events.append((1.7 * min(q, ring_y - q) + 1.8, 2, q, q))
+        for when, kind, d, slot in sorted(events):
+            if kind == 0:
+                chunk = src_chunk(x * ring_y + (y + ring_y - d) % ring_y)
+                wait_bytes(chunk, y_recv.at[slot])
+                pass_on(chunk, y_step, ring_y, d, gather_send.at[0], y_recv)
+                hand_out(chunk, (ring_y - d) % ring_y)
+            elif kind == 1:
+                chunk = tgt_chunk((z + ring_z - d) % ring_z * CORES + core)
+                wait_bytes(chunk, z_recv.at[slot])
+                pass_on(chunk, z_step, ring_z, d, gather_send.at[1], z_recv)
                 send(chunk, chunk, gather_send.at[3], pair_recv, partner)
             else:
-                chunk = src_chunk(x * ring_y + (y + ring_y - y_offsets[k]) % ring_y)
-                wait_bytes(chunk, y_recv.at[k])
-                for peer in x_peers:
-                    send(chunk, chunk, gather_send.at[2], x_recv, peer)
+                way = 1 if d % 2 == 0 else -1
+                owner_x = (x + ring_x - way) % ring_x
+                chunk = src_chunk(owner_x * ring_y + (y + d) % ring_y)
+                wait_bytes(chunk, x_relay.at[slot])
+                send(chunk, chunk, gather_send.at[2], x_recv, x_step(way))
 
         wait_bytes(gtgt.at[pl.ds(0, ring_z * tgt_size)], pair_recv)
         operands(gtgt, right, tgt_rows, 1.0, False)
-        wait_bytes(gsrc.at[pl.ds(0, len(x_peers) * ring_y * src_size)], x_recv)
+        wait_bytes(gsrc.at[pl.ds(0, rest_chunks * src_size)], x_recv)
         operands(gsrc, left, src_rows, -2.0 * unit, True)
         fill(cost_t, right, left, 1, tiles)
 
@@ -397,9 +425,10 @@
 
         lax.fori_loop(0, ITERS, iterate, zero)
 
-        wait_bytes(gsrc.at[pl.ds(0, len(y_peers) * src_size)], gather_send.at[0])
-        wait_bytes(gtgt.at[pl.ds(0, len(chain_peers) * tgt_size)], gather_send.at[1])
-        wait_bytes(gsrc.at[pl.ds(0, len(x_peers) * ring_y * src_size)], gather_send.at[2])
+        wait_bytes(gsrc.at[pl.ds(0, (ring_y - 1) * src_size)], gather_send.at[0])
+        if ring_z > 1:
+            wait_bytes(gtgt.at[pl.ds(0, (ring_z - 1) * tgt_size)], gather_send.at[1])
+        wait_bytes(gsrc.at[pl.ds(0, (ring_x - 1) * ring_y * src_size)], gather_send.at[2])
         wait_bytes(gtgt.at[pl.ds(0, ring_z * tgt_size)], gather_send.at[3])
         wait_bytes(far_row, row_send.at[0])
         wait_bytes(near_row, row_send.at[1])
@@ -437,9 +466,10 @@
         near_slots(z_near),
         pltpu.SemaphoreType.DMA((6,)),
         pltpu.SemaphoreType.DMA((4,)),
-        pltpu.SemaphoreType.DMA((len(y_offsets),)),
-        pltpu.SemaphoreType.DMA((len(chain_offsets),)),
+        pltpu.SemaphoreType.DMA((ring_y,)),
+        pltpu.SemaphoreType.DMA((ring_z,)),
         pltpu.SemaphoreType.DMA,
+        pltpu.SemaphoreType.DMA((ring_y,)),
         pltpu.SemaphoreType.DMA,
         pltpu.SemaphoreType.DMA((2,)),
         pltpu.SemaphoreType.DMA((2,)),

time: 70.2 us -> 76.6 us (1.091)
  Pallas kernels: 68.1 us -> 74.5 us
    pallas_call x1, Pallas kernels: 68.1 us -> 74.5 us  [shards(): pl.pallas_call(kernel, out_shape=(side, side), in_specs=[pl.BlockSpec(mem...]
where the time goes in v5:
time: 76.6 us; the launch traced here: 76.4 us
  Pallas kernels  74.5 us (97%)
  between operations  1.29 us (2%)
    pallas_call x1, Pallas kernels, shards(): pl.pallas_call(kernel, out_shape=(side, side), in_specs=[pl.BlockSpec(mem...  74.5 us

profile of v5, /device:TPU:1, one launch (start us, length us, event | category | flops | bytes accessed | tf_op | source)
XLA Modules:
  0.0 76.4 jit_solution(14995719757886149460)
XLA Ops:
  1.3 74.5 %sinkhorn.1 = (f32[8,128]{1,0:T(8,128)S(1)}, f32[8,128]{1,0:T(8,128)S(1)}) custom-call(f32[2,1024]{1,0:T(2,128)} %src_hbm.1, f32[4,1024]{1,0:T(4,128)} %tgt_hbm.1, f32[8,128]{1,0:T(8,128)} %bitcast.6, f32[8,128]{1,0:T(8,128)} %bitcast.7, s32[1,1,2,12]{3,2,1,0:T(2,128)} %list_hbm.1, s32[1,1]{1,0:T(1,128)S(6)} %copy.8.count_hbm), custom_call_target="tpu_custom_call" | custom-call | tf_op jit(solution)/shard_map/sinkhorn/pallas_call | solution.py:490
  75.8 0.6 multiply_bitcast_fusion

commit v6 on v4

--- a/solution.py
+++ b/solution.py
@@ -61,7 +61,6 @@
     y_offsets = ring_offsets(ring_y)
     z_offsets = [(0, 1)] + [(dz, dc) for dz in range(1, ring_z) for dc in range(CORES)]
     z_offsets.sort(key=lambda o: -min(o[0], ring_z - o[0]))
-    chain_offsets = ring_offsets(ring_z)
     def reach_of(dx, dy):
         return min(dx, ring_x - dx) + min(dy, ring_y - dy)
 
@@ -107,7 +106,6 @@
         y_recv,
         z_recv,
         x_recv,
-        pair_recv,
         row_send,
         col_send,
         far_row_recv,
@@ -121,8 +119,6 @@
         z, core = row // CORES, row % CORES
         x_peers = [(row, (x + dx) % ring_x * ring_y + y) for dx in x_offsets]
         y_peers = [(row, x * ring_y + (y + dy) % ring_y) for dy in y_offsets]
-        chain_peers = [((z + dz) % ring_z * CORES + core, col) for dz in chain_offsets]
-        partner = (z * CORES + (core + 1) % CORES, col)
         z_peers = [((z + dz) % ring_z * CORES + (core + dc) % CORES, col) for dz, dc in z_offsets]
         plane_peers = [
             (row, (x + dx) % ring_x * ring_y + (y + dy) % ring_y) for dx, dy in plane_offsets
@@ -174,13 +170,10 @@
                 device_id_type=MESH,
             ).start()
 
-        for k, peer in enumerate(y_peers):
-            send(own_src, own_src, gather_send.at[0], y_recv.at[k], peer)
-        for k, peer in enumerate(chain_peers):
-            send(own_tgt, own_tgt, gather_send.at[1], z_recv.at[k], peer)
-        for peer in x_peers:
-            send(own_src, own_src, gather_send.at[2], x_recv, peer)
-        send(own_tgt, own_tgt, gather_send.at[3], pair_recv, partner)
+        for peer in y_peers:
+            send(own_src, own_src, gather_send.at[0], y_recv, peer)
+        for peer in z_peers:
+            send(own_tgt, own_tgt, gather_send.at[1], z_recv, peer)
 
         slots = list_ref[0, 0]
         tile_ids = (slots[0:1, :] - row * tiles) * tiles + (slots[1:2, :] - col * tiles)
@@ -315,20 +308,12 @@
                 for k, peer in enumerate(peers[far_count:]):
                     send(own.at[turn], near.at[turn, k], sends.at[1], near_recv.at[turn], peer)
 
-        arrivals = [(min(d, ring_y - d), 0, k) for k, d in enumerate(y_offsets)]
-        arrivals += [(min(d, ring_z - d) + 1.5, 1, k) for k, d in enumerate(chain_offsets)]
-        for when, chain, k in sorted(arrivals):
-            if chain:
-                chunk = tgt_chunk((z + ring_z - chain_offsets[k]) % ring_z * CORES + core)
-                wait_bytes(chunk, z_recv.at[k])
-                send(chunk, chunk, gather_send.at[3], pair_recv, partner)
-            else:
-                chunk = src_chunk(x * ring_y + (y + ring_y - y_offsets[k]) % ring_y)
-                wait_bytes(chunk, y_recv.at[k])
-                for peer in x_peers:
-                    send(chunk, chunk, gather_send.at[2], x_recv, peer)
-
-        wait_bytes(gtgt.at[pl.ds(0, ring_z * tgt_size)], pair_recv)
+        wait_bytes(gsrc.at[pl.ds(0, len(y_peers) * src_size)], y_recv)
+        group = ring_y * src_size
+        own_group = gsrc.at[pl.ds(pl.multiple_of(x * group, group), group)]
+        for peer in x_peers:
+            send(own_group, own_group, gather_send.at[2], x_recv, peer)
+        wait_bytes(gtgt.at[pl.ds(0, len(z_peers) * tgt_size)], z_recv)
         operands(gtgt, right, tgt_rows, 1.0, False)
         wait_bytes(gsrc.at[pl.ds(0, len(x_peers) * ring_y * src_size)], x_recv)
         operands(gsrc, left, src_rows, -2.0 * unit, True)
@@ -398,9 +383,8 @@
         lax.fori_loop(0, ITERS, iterate, zero)
 
         wait_bytes(gsrc.at[pl.ds(0, len(y_peers) * src_size)], gather_send.at[0])
-        wait_bytes(gtgt.at[pl.ds(0, len(chain_peers) * tgt_size)], gather_send.at[1])
+        wait_bytes(gtgt.at[pl.ds(0, len(z_peers) * tgt_size)], gather_send.at[1])
         wait_bytes(gsrc.at[pl.ds(0, len(x_peers) * ring_y * src_size)], gather_send.at[2])
-        wait_bytes(gtgt.at[pl.ds(0, ring_z * tgt_size)], gather_send.at[3])
         wait_bytes(far_row, row_send.at[0])
         wait_bytes(near_row, row_send.at[1])
         wait_bytes(far_col, col_send.at[0])
@@ -436,9 +420,8 @@
         near_slots(plane_near),
         near_slots(z_near),
         pltpu.SemaphoreType.DMA((6,)),
-        pltpu.SemaphoreType.DMA((4,)),
-        pltpu.SemaphoreType.DMA((len(y_offsets),)),
-        pltpu.SemaphoreType.DMA((len(chain_offsets),)),
+        pltpu.SemaphoreType.DMA((3,)),
+        pltpu.SemaphoreType.DMA,
         pltpu.SemaphoreType.DMA,
         pltpu.SemaphoreType.DMA,
         pltpu.SemaphoreType.DMA((2,)),

time: 70.2 us -> 69.9 us (level)
  no operation moved by 1% of the time
where the time goes in v6:
time: 69.9 us; the launch traced here: 69.7 us
  Pallas kernels  67.8 us (97%)
  between operations  1.29 us (2%)
    pallas_call x1, Pallas kernels, shards(): pl.pallas_call(kernel, out_shape=(side, side), in_specs=[pl.BlockSpec(mem...  67.8 us

profile of v6, /device:TPU:1, one launch (start us, length us, event | category | flops | bytes accessed | tf_op | source)
XLA Modules:
  0.0 69.7 jit_solution(5530288394926521434)
XLA Ops:
  1.3 67.8 %sinkhorn.1 = (f32[8,128]{1,0:T(8,128)S(1)}, f32[8,128]{1,0:T(8,128)S(1)}) custom-call(f32[2,1024]{1,0:T(2,128)} %src_hbm.1, f32[4,1024]{1,0:T(4,128)} %tgt_hbm.1, f32[8,128]{1,0:T(8,128)} %bitcast.6, f32[8,128]{1,0:T(8,128)} %bitcast.7, s32[1,1,2,12]{3,2,1,0:T(2,128)} %list_hbm.1, s32[1,1]{1,0:T(1,128)S(6)} %copy.8.count_hbm), custom_call_target="tpu_custom_call" | custom-call | tf_op jit(solution)/shard_map/sinkhorn/pallas_call | solution.py:443
  69.1 0.6 multiply_bitcast_fusion

commit v7 on v6

--- a/solution.py
+++ b/solution.py
@@ -13,7 +13,7 @@
 RING_Y = 8
 CORES = 2
 SPAN = 64
-UNROLL = 4
+UNROLL = 8
 HALVES = 2
 
 entropic = 0.1

time: 69.9 us -> 69.2 us (0.990)
  Pallas kernels: 67.8 us -> 67.1 us
where the time goes in v7:
time: 69.2 us; the launch traced here: 69 us
  Pallas kernels  67.1 us (97%)
  between operations  1.29 us (2%)
    pallas_call x1, Pallas kernels, shards(): pl.pallas_call(kernel, out_shape=(side, side), in_specs=[pl.BlockSpec(mem...  67.1 us

profile of v7, /device:TPU:1, one launch (start us, length us, event | category | flops | bytes accessed | tf_op | source)
XLA Modules:
  0.0 69.0 jit_solution(1583435645136687998)
XLA Ops:
  1.3 67.1 %sinkhorn.1 = (f32[8,128]{1,0:T(8,128)S(1)}, f32[8,128]{1,0:T(8,128)S(1)}) custom-call(f32[2,1024]{1,0:T(2,128)} %src_hbm.1, f32[4,1024]{1,0:T(4,128)} %tgt_hbm.1, f32[8,128]{1,0:T(8,128)} %bitcast.6, f32[8,128]{1,0:T(8,128)} %bitcast.7, s32[1,1,2,12]{3,2,1,0:T(2,128)} %list_hbm.1, s32[1,1]{1,0:T(1,128)S(6)} %copy.8.count_hbm), custom_call_target="tpu_custom_call" | custom-call | tf_op jit(solution)/shard_map/sinkhorn/pallas_call | solution.py:443
  68.4 0.6 multiply_bitcast_fusion
